TPU v7x, 128 devices: a whole 4x4x4 slice. The times are simulated.
128 devices in a mesh: row: 8 (over x_lo, z), col: 16 (over x_hi, y, core).
Axes of the slice: x: 4 (x_hi: 2, x_lo: 2; x = x_hi * 2 + x_lo), y: 4, z: 4, core: 2. Of those that a mesh axis runs over, the one named last changes fastest.
Arguments:
- tokens: bfloat16 [2048, 4096], P('row', 'col'), may hold values from -6 to 6
- norm_gain: float32 [4096], replicated, may hold values from 0.1 to 1.9
- expert_ids: int32 [2048, 2], P('row'), may hold values from 0 to 7, all different within a row; in each aligned block of 256 rows (0 to 255, 256 to 511, ...) at most 128 rows name the same one
- gate_weights: float32 [2048, 2], P('row'), may hold values from 0.1 to 1
- w_gate: bfloat16 [8, 4096, 14336], P('row', None, 'col'), may hold values from -0.09375 to 0.09375
- w_up: bfloat16 [8, 4096, 14336], P('row', None, 'col'), may hold values from -0.09375 to 0.09375
- w_down: bfloat16 [8, 14336, 4096], P('row', 'col'), may hold values from -0.046875 to 0.046875
Outputs:
- layer_output: bfloat16 [2048, 4096], P('row', 'col')
Inputs may be any that keep to these rules, and one draw needn't show every extreme that they name: `expert_ids`: the 2 experts of a token differ. In each aligned block of 256 tokens no expert is chosen by more than 128 tokens, a bound that some block reaches.
All inputs are finite; a program needn't handle non-finite values.
Results may differ from a plain program's by a relative error of at most 0.0043.
Values may be sent and summed in bfloat16 or wider, within the bound.
A program may use at most 128 MiB of HBM per device.

v0:
```python
import jax
import jax.numpy as jnp
from jax import lax
from jax.sharding import Mesh
from jax.sharding import PartitionSpec as P

EXPERTS = 8
CAP = 128
COL = ("chip", "core")


def route_tables(expert_ids, expert_count, capacity):
    token_count = expert_ids.shape[0]
    flat_ids = expert_ids.reshape(-1)
    expert_range = jnp.arange(expert_count, dtype=jnp.int32)
    expert_hits = (flat_ids[:, None] == expert_range[None, :]).astype(jnp.int32)
    earlier = jnp.cumsum(expert_hits, axis=0) - expert_hits
    ranks = jnp.sum(earlier * expert_hits, axis=1)
    slot_index = (flat_ids * capacity + ranks).reshape(token_count, -1)
    slot_ids = jnp.arange(expert_count * capacity, dtype=jnp.int32)
    matches = (slot_index[:, :, None] == slot_ids[None, None, :]).astype(jnp.float32)
    picker = jnp.sum(matches, axis=1)
    return (picker.astype(jnp.bfloat16), slot_index)


def combine_rows(slot_rows, slot_index, gate_weights):
    picked = slot_rows[slot_index]
    return jnp.sum(picked * gate_weights[:, :, None], axis=1)


def swap_cores(value):
    return lax.ppermute(value, "core", perm=[(0, 1), (1, 0)])


def body(tokens, norm_gain, expert_ids, gate_weights, w_gate, w_up, w_down):
    chips = lax.psum(1, "chip")
    width = tokens.shape[1]
    core = lax.axis_index("core")
    block = lax.axis_index("chip") * 2 + core
    values = tokens.astype(jnp.float32)
    squares = lax.psum(jnp.sum(values * values, axis=-1, keepdims=True), COL)
    inverse_norm = lax.rsqrt(squares / (width * chips * 2) + 1e-05)
    gain = lax.dynamic_slice_in_dim(norm_gain, block * width, width)
    normed = (values * inverse_norm * gain).astype(jnp.bfloat16)
    picker, slot_index = route_tables(expert_ids, EXPERTS, CAP)
    packed = jnp.einsum("ts,td->sd", picker, normed, preferred_element_type=jnp.float32).astype(
        jnp.bfloat16
    )
    packed = packed.reshape(EXPERTS, CAP, width)
    arrived = lax.all_to_all(packed, "row", split_axis=0, concat_axis=0, tiled=True)
    arrived = arrived.reshape(EXPERTS * CAP, width)
    mine = lax.all_gather(arrived, "chip", axis=0, tiled=False)
    other = swap_cores(mine)
    pair = jnp.where(core == 0, jnp.stack([mine, other], 1), jnp.stack([other, mine], 1))
    slots = arrived.shape[0]
    widened = jnp.transpose(pair, (2, 0, 1, 3)).reshape(slots, chips * 2 * width)
    gate_part = jnp.dot(widened, w_gate[0], preferred_element_type=jnp.float32)
    up_part = jnp.dot(widened, w_up[0], preferred_element_type=jnp.float32)
    hidden = (jax.nn.silu(gate_part) * up_part).astype(jnp.bfloat16)
    outputs = jnp.dot(hidden, w_down[0], preferred_element_type=jnp.float32)
    split = outputs.reshape(slots, chips, 2, width)
    keep = jnp.where(core == 0, split[:, :, 0], split[:, :, 1])
    give = jnp.where(core == 0, split[:, :, 1], split[:, :, 0])
    summed = keep + swap_cores(give)
    shares = lax.psum_scatter(summed, "chip", scatter_dimension=1, tiled=True)
    shares = shares.reshape(EXPERTS, CAP, width)
    returned = lax.all_to_all(shares, "row", split_axis=0, concat_axis=0, tiled=True)
    mixed = combine_rows(returned.reshape(-1, width), slot_index, gate_weights)
    return (tokens.astype(jnp.float32) + mixed).astype(jnp.bfloat16)


def solution(mesh):
    rows, cols = mesh.devices.shape
    split_mesh = Mesh(mesh.devices.reshape(rows, cols // 2, 2), ("row", "chip", "core"))
    placed = (
        P("row", COL),
        P(),
        P("row", None),
        P("row", None),
        P("row", None, COL),
        P("row", None, COL),
        P("row", COL, None),
    )
    return jax.shard_map(
        body, mesh=split_mesh, in_specs=placed, out_specs=P("row", COL), check_vma=False
    )
```

profile of v0, /device:TPU:0, one launch (start us, length us, event | category | flops | bytes accessed | tf_op | source)
XLA Modules:
  0.0 370.8 jit_solution(8695487437753940584)
XLA Ops:
  6.5 0.8 copy.51
  7.7 1.1 reduce-window.6
  9.4 0.7 compare_select_fusion
  10.4 1.0 fusion.9
  11.4 38.1 %psum.7 = f32[256,1]{0,1:T(1,128)S(1)} all-reduce(f32[256,1]{0,1:T(1,128)S(1)} %bitcast.67), channel_id=1, replica_groups=mesh['row'=8,'chip'=8,'core'=2] {'chip','core'}, use_global_device_ids=true, to_apply=%region_5.6 | all-reduce | flops 256 | bytes 2048 | tf_op jit(solution)/shard_map/psum | solution.py:41
  49.5 0.8 dynamic_slice.3
  50.3 1.3 convolution_convert_fusion
  51.6 13.9 %all_to_all.10 = bf16[8,128,256]{2,1,0:T(8,128)(2,1)} all-to-all(bf16[8,128,256]{2,1,0:T(8,128)(2,1)S(1)} %bitcast.66), channel_id=1, replica_groups=mesh['row'=8,'chip'=8,'core'=2] {'row'}, dimensions={0} | all-to-all | bytes 1048576 | tf_op jit(solution)/shard_map/all_to_all | solution.py:50
  65.5 67.0 %all-gather.2.cloned.1.call-done = bf16[8,1024,256]{2,1,0:T(8,128)(2,1)} async-done(((bf16[1,1024,256]{2,1,0:T(8,128)(2,1)}), bf16[8,1024,256]{2,1,0:T(8,128)(2,1)}) %all-gather.2.cloned.1.call-update) | async-done | bytes 4194320 | tf_op jit(solution)/shard_map/all_gather | solution.py:52
  132.6 6.4 %copy.54 = bf16[8,1024,256]{1,2,0:T(8,128)(2,1)} copy(bf16[8,1024,256]{2,1,0:T(8,128)(2,1)} %all-gather.2.cloned.1.call-done) | data formatting | bytes 8388608 | tf_op jit(solution)/shard_map/all_gather | solution.py:52
  139.0 10.8 %copy.64 = bf16[4096,896]{1,0:T(8,128)(2,1)} copy(bf16[4096,896]{0,1:T(8,128)(2,1)} %bitcast.60) | data formatting | bytes 14680064 | tf_op jit(solution)/shard_map/dot_general | solution.py:60
  149.8 7.9 %maximum_select_fusion = bf16[8,2,1024,256]{2,3,1,0:T(8,128)(2,1)S(1)} fusion(bf16[8,1,1024,256]{2,3,1,0:T(8,128)(2,1)} %bitcast.7, bf16[8,1,1024,256]{2,3,1,0:T(8,128)(2,1)} %bitcast.57, pred[]{:T(512)S(6)} %eq.43), kind=kLoop, calls=%fused_computation.1 | loop fusion | flops 12582912 | bytes 16777216 | tf_op jit(solution)/shard_map/jit(_where)/select_n | solution.py:54
  157.8 13.0 %fusion.2 = f32[1024,896]{1,0:T(8,128)S(1)} fusion(bf16[1024,4096]{0,1:T(8,128)(2,1)S(1)} %bitcast.58, bf16[1,4096,896]{2,1,0:T(8,128)(2,1)} %param.12), kind=kOutput, calls=%fused_computation.6 | convolution fusion | flops 7516192768 | bytes 19398656 | tf_op jit(solution)/shard_map/dot_general | solution.py:58
  170.9 11.1 %fusion.4 = f32[1024,896]{1,0:T(8,128)} fusion(bf16[1024,4096]{0,1:T(8,128)(2,1)S(1)} %bitcast.59, bf16[1,4096,896]{2,1,0:T(8,128)(2,1)S(1)} %bitcast.70), kind=kOutput, calls=%fused_computation.8 | convolution fusion | flops 7516192768 | bytes 19398656 | tf_op jit(solution)/shard_map/dot_general | solution.py:57
  182.0 13.8 %fusion.6 = f32[1024,8,2,256]{3,0,2,1:T(8,128)} fusion(bf16[8,2,256,896]{3,2,1,0:T(8,128)(2,1)S(1)} %bitcast.63, f32[1024,896]{1,0:T(8,128)S(1)} %fusion.2, f32[1024,896]{1,0:T(8,128)} %fusion.4), kind=kOutput, calls=%fused_computation.13 | convolution fusion | flops 7521697792 | bytes 31457280 | tf_op jit(solution)/shard_map/dot_general | solution.py:60
  195.8 10.1 %select_bitcast_fusion = f32[1024,8,256]{2,0,1:T(8,128)} fusion(f32[1024,8,2,256]{3,0,2,1:T(8,128)} %fusion.6, pred[]{:T(512)S(6)} %eq.43), kind=kLoop, calls=%fused_computation.5 | loop fusion | flops 2097152 | bytes 25165824 | tf_op jit(solution)/shard_map/jit(_where)/select_n | solution.py:63
  206.3 13.0 %collective-permute-done.1 = f32[1024,8,256]{2,0,1:T(8,128)S(1)} collective-permute-done((f32[1024,8,256]{2,0,1:T(8,128)}, f32[1024,8,256]{2,0,1:T(8,128)S(1)}, u32[]{:S(2)}, u32[]{:S(2)}) %collective-permute-start.1) | collective-permute-done | bytes 8388640 | tf_op jit(solution)/shard_map/ppermute | solution.py:32
  219.3 10.0 %fusion.1 = f32[1024,8,256]{2,0,1:T(8,128)} fusion(f32[1024,8,256]{2,0,1:T(8,128)S(1)} %collective-permute-done.1, f32[1024,8,2,256]{3,0,2,1:T(8,128)} %fusion.6, pred[]{:T(512)S(6)} %eq.43), kind=kLoop, calls=%fused_computation.4 | loop fusion | flops 4194304 | bytes 33554432 | tf_op jit(solution)/shard_map/add | solution.py:64
  229.4 112.7 %reduce-scatter.2.cloned.1.call-done = f32[1024,1,256]{2,0,1:T(8,128)} async-done(((f32[1024,8,256]{2,0,1:T(8,128)}), f32[1024,1,256]{2,0,1:T(8,128)}) %reduce-scatter.2.cloned.1.call-update) | async-done | bytes 1048592 | tf_op jit(solution)/shard_map/reduce_scatter | solution.py:65
  342.1 4.4 %all-to-all-start.1 = ((f32[8,128,256]{2,1,0:T(8,128)}), f32[8,128,256]{2,1,0:T(8,128)S(1)}, u32[]{:S(2)}, u32[]{:S(2)}) async-start(f32[8,128,256]{2,1,0:T(8,128)} %bitcast.65), calls=%async_computation.2 | async-start | bytes 2097152 | tf_op jit(solution)/shard_map/all_to_all | solution.py:67
  347.0 13.7 %all-to-all-done.1 = f32[8,128,256]{2,1,0:T(8,128)S(1)} async-done(((f32[8,128,256]{2,1,0:T(8,128)}), f32[8,128,256]{2,1,0:T(8,128)S(1)}, u32[]{:S(2)}, u32[]{:S(2)}) %all-to-all-start.1) | async-done | bytes 1048608 | tf_op jit(solution)/shard_map/all_to_all | solution.py:67
  360.7 1.6 gather_fusion
  362.6 0.7 multiply_reduce_fusion
  363.3 0.7 fusion.12
  (37 shorter events, 2.5 us)
Async XLA Ops:
  6.5 126.0 %all-gather.2.cloned.1.call-start = ((), (), s32[]{:S(2)}) async-start(), calls=%async_computation.3 | async-start | bytes 4718592 | tf_op jit(solution)/shard_map/all_gather | solution.py:52
  65.5 276.6 %reduce-scatter.2.cloned.1.call-start = ((), (), s32[]{:S(2)}) async-start(), calls=%async_computation.4 | async-start | bytes 9437184 | tf_op jit(solution)/shard_map/reduce_scatter | solution.py:65
  139.0 10.8 %collective-permute-start = (bf16[8,1024,256]{1,2,0:T(8,128)(2,1)}, bf16[8,1024,256]{1,2,0:T(8,128)(2,1)}, u32[]{:S(2)}, u32[]{:S(2)}) collective-permute-start(bf16[8,1024,256]{1,2,0:T(8,128)(2,1)} %copy.54), channel_id=1, source_target_pairs={{0,1},{1,0},{2,3},{3,2},{4,5},{5,4},{6,7},{7,6},{8,9},{9,8},{10,11... | collective-permute-start | bytes 12582920 | tf_op jit(solution)/shard_map/ppermute | solution.py:32
  149.8 21.0 %slice-start.2 = ((s8[7340032]{0:T(1024)(128)(4,1)}), s8[4194304]{0:T(1024)(128)(4,1)S(1)}, s32[]{:S(2)}) async-start(s8[7340032]{0:T(1024)(128)(4,1)} %bitcast.69), calls=%async_computation.7 | async-start | bytes 8388608
  157.8 13.1 %slice-start.3 = ((s8[7340032]{0:T(1024)(128)(4,1)}), s8[3145728]{0:T(1024)(128)(4,1)S(1)}, s32[]{:S(2)}) async-start(s8[7340032]{0:T(1024)(128)(4,1)} %bitcast.69), calls=%async_computation.8 | async-start | bytes 6291456
  157.8 24.2 %slice-start = ((s8[7340032]{0:T(1024)(128)(4,1)}), s8[4194304]{0:T(1024)(128)(4,1)S(1)}, s32[]{:S(2)}) async-start(s8[7340032]{0:T(1024)(128)(4,1)} %bitcast.61), calls=%async_computation.5 | async-start | bytes 8388608
  170.9 11.1 %slice-start.1 = ((s8[7340032]{0:T(1024)(128)(4,1)}), s8[3145728]{0:T(1024)(128)(4,1)S(1)}, s32[]{:S(2)}) async-start(s8[7340032]{0:T(1024)(128)(4,1)} %bitcast.61), calls=%async_computation.6 | async-start | bytes 6291456
  205.8 13.5 %collective-permute-start.1 = (f32[1024,8,256]{2,0,1:T(8,128)}, f32[1024,8,256]{2,0,1:T(8,128)S(1)}, u32[]{:S(2)}, u32[]{:S(2)}) collective-permute-start(f32[1024,8,256]{2,0,1:T(8,128)} %select_bitcast_fusion), channel_id=1, source_target_pairs={{0,1},{1,0},{2,3},{3,2},{4,5},{5,4},{6,7},{7,6},{8,9},{9,8},{10,11... | collective-permute-start | bytes 25165832 | tf_op jit(solution)/shard_map/ppermute | solution.py:32
  229.3 117.4 %copy-start.1 = (f32[256,2]{0,1:T(2,128)S(1)}, f32[256,2]{0,1:T(2,128)}, u32[]{:S(2)}) copy-start(f32[256,2]{0,1:T(2,128)} %param.10) | copy-start | bytes 6148
  229.3 134.0 %copy-start = (bf16[256,256]{1,0:T(8,128)(2,1)S(1)}, bf16[256,256]{1,0:T(8,128)(2,1)}, u32[]{:S(2)}) copy-start(bf16[256,256]{1,0:T(8,128)(2,1)} %param.7) | copy-start | bytes 393220
  342.1 18.6 %all-to-all-start.1 = ((f32[8,128,256]{2,1,0:T(8,128)}), f32[8,128,256]{2,1,0:T(8,128)S(1)}, u32[]{:S(2)}, u32[]{:S(2)}) async-start(f32[8,128,256]{2,1,0:T(8,128)} %bitcast.65), calls=%async_computation.2 | async-start | bytes 2097152 | tf_op jit(solution)/shard_map/all_to_all | solution.py:67
Sparse Core Ops, SparseCore 0:
  65.6 66.8 all-gather.1
  229.5 112.5 reduce-scatter.1
where the time goes:
time: 372 us; the launch traced here: 371 us
  waiting for transfers between devices  206 us (55%)
  blocking collectives  52 us (14%)
  matrix products  39.2 us (11%)
  other arithmetic  32.7 us (9%)
  local copies, waits for them, and re-layouts  21.9 us (6%)
  between operations  13.6 us (4%)
  starting transfers between devices  4.98 us (1%)
    reduce_scatter x1, waiting for transfers between devices, body(): shares = lax.psum_scatter(summed, 'chip', scatter_dimension=1, tiled=True)  113 us
    all_gather x1, waiting for transfers between devices, body(): mine = lax.all_gather(arrived, 'chip', axis=0, tiled=False)  67 us
    psum x1, blocking collectives, body(): squares = lax.psum(jnp.sum(values * values, axis=-1, keepdims=True), COL)  38.1 us
    all_to_all x1, blocking collectives, body(): lax.all_to_all(packed, 'row', split_axis=0, concat_axis=0, tiled=True)  13.9 us
    dot_general x1, matrix products, body(): outputs = jnp.dot(hidden, w_down[0], preferred_element_type=jnp.float32)  13.8 us
    all_to_all x1, waiting for transfers between devices, body(): lax.all_to_all(shares, 'row', split_axis=0, concat_axis=0, tiled=True)  13.7 us
    dot_general x1, matrix products, body(): up_part = jnp.dot(widened, w_up[0], preferred_element_type=jnp.float32)  13 us
    ppermute x2, waiting for transfers between devices, swap_cores(): return lax.ppermute(value, 'core', perm=[(0, 1), (1, 0)])  13 us
  transfers between devices with their start and end apart: 5, of which 4 were waited for; matrix products, arithmetic and copies ran while one was open for 3% of the time, Pallas kernels for 0%

commit v1 on v0

--- a/solution.py
+++ b/solution.py
@@ -38,7 +38,9 @@
     core = lax.axis_index("core")
     block = lax.axis_index("chip") * 2 + core
     values = tokens.astype(jnp.float32)
-    squares = lax.psum(jnp.sum(values * values, axis=-1, keepdims=True), COL)
+    squares = jax.lax.psum(
+        jax.lax.psum(jnp.sum(values * values, axis=-1, keepdims=True), "core"), "chip"
+    )
     inverse_norm = lax.rsqrt(squares / (width * chips * 2) + 1e-05)
     gain = lax.dynamic_slice_in_dim(norm_gain, block * width, width)
     normed = (values * inverse_norm * gain).astype(jnp.bfloat16)

time: 372 us -> 360 us (0.968)
  blocking collectives: 52 us -> 40.8 us
    psum x1 -> x2, blocking collectives: 38.1 us -> 27 us  [the longest x1 24.5 us: body(): jax.lax.psum(jax.lax.psum(jnp.sum(values * values, axis=-1, keepdims=True...]
where the time goes in v1:
time: 360 us
  waiting for transfers between devices  206 us (57%)
  blocking collectives  40.8 us (11%)
  matrix products  39.2 us (11%)
  other arithmetic  32.7 us (9%)
  local copies, waits for them, and re-layouts  21.9 us (6%)
  between operations  13.6 us (4%)
  starting transfers between devices  4.98 us (1%)
    reduce_scatter x1, waiting for transfers between devices, body(): shares = lax.psum_scatter(summed, 'chip', scatter_dimension=1, tiled=True)  113 us
    all_gather x1, waiting for transfers between devices, body(): mine = lax.all_gather(arrived, 'chip', axis=0, tiled=False)  67 us
    psum x1, blocking collectives, body(): jax.lax.psum(jax.lax.psum(jnp.sum(values * values, axis=-1, keepdims=True...  24.5 us
    all_to_all x1, blocking collectives, body(): lax.all_to_all(packed, 'row', split_axis=0, concat_axis=0, tiled=True)  13.9 us
    dot_general x1, matrix products, body(): outputs = jnp.dot(hidden, w_down[0], preferred_element_type=jnp.float32)  13.8 us
    all_to_all x1, waiting for transfers between devices, body(): lax.all_to_all(shares, 'row', split_axis=0, concat_axis=0, tiled=True)  13.7 us
    dot_general x1, matrix products, body(): up_part = jnp.dot(widened, w_up[0], preferred_element_type=jnp.float32)  13 us
    ppermute x2, waiting for transfers between devices, swap_cores(): return lax.ppermute(value, 'core', perm=[(0, 1), (1, 0)])  13 us
  transfers between devices with their start and end apart: 5, of which 4 were waited for; matrix products, arithmetic and copies ran while one was open for 3% of the time, Pallas kernels for 0%

profile of v1, /device:TPU:0, one launch (start us, length us, event | category | flops | bytes accessed | tf_op | source)
XLA Modules:
  0.0 359.7 jit_solution(14562715813988002859)
XLA Ops:
  6.5 0.8 copy.51
  7.7 1.1 reduce-window.6
  9.4 0.7 compare_select_fusion
  10.4 1.0 fusion.9
  11.4 2.5 psum.14
  13.8 24.5 %psum.15 = f32[256,1]{0,1:T(1,128)S(1)} all-reduce(f32[256,1]{0,1:T(1,128)S(1)} %psum.14), channel_id=1, replica_groups=mesh['row'=8,'chip'=8,'core'=2] {'chip'}, use_global_device_ids=true, to_apply=%region_6.7 | all-reduce | flops 256 | bytes 2048 | tf_op jit(solution)/shard_map/psum | solution.py:41
  38.3 0.8 dynamic_slice.3
  39.1 1.3 convolution_convert_fusion
  40.4 13.9 %all_to_all.10 = bf16[8,128,256]{2,1,0:T(8,128)(2,1)} all-to-all(bf16[8,128,256]{2,1,0:T(8,128)(2,1)S(1)} %bitcast.66), channel_id=1, replica_groups=mesh['row'=8,'chip'=8,'core'=2] {'row'}, dimensions={0} | all-to-all | bytes 1048576 | tf_op jit(solution)/shard_map/all_to_all | solution.py:52
  54.4 67.0 %all-gather.2.cloned.1.call-done = bf16[8,1024,256]{2,1,0:T(8,128)(2,1)} async-done(((bf16[1,1024,256]{2,1,0:T(8,128)(2,1)}), bf16[8,1024,256]{2,1,0:T(8,128)(2,1)}) %all-gather.2.cloned.1.call-update) | async-done | bytes 4194320 | tf_op jit(solution)/shard_map/all_gather | solution.py:54
  121.4 6.4 %copy.54 = bf16[8,1024,256]{1,2,0:T(8,128)(2,1)} copy(bf16[8,1024,256]{2,1,0:T(8,128)(2,1)} %all-gather.2.cloned.1.call-done) | data formatting | bytes 8388608 | tf_op jit(solution)/shard_map/all_gather | solution.py:54
  127.8 10.8 %copy.64 = bf16[4096,896]{1,0:T(8,128)(2,1)} copy(bf16[4096,896]{0,1:T(8,128)(2,1)} %bitcast.60) | data formatting | bytes 14680064 | tf_op jit(solution)/shard_map/dot_general | solution.py:62
  138.7 7.9 %maximum_select_fusion = bf16[8,2,1024,256]{2,3,1,0:T(8,128)(2,1)S(1)} fusion(bf16[8,1,1024,256]{2,3,1,0:T(8,128)(2,1)} %bitcast.7, bf16[8,1,1024,256]{2,3,1,0:T(8,128)(2,1)} %bitcast.57, pred[]{:T(512)S(6)} %eq.43), kind=kLoop, calls=%fused_computation.1 | loop fusion | flops 12582912 | bytes 16777216 | tf_op jit(solution)/shard_map/jit(_where)/select_n | solution.py:56
  146.6 13.0 %fusion.2 = f32[1024,896]{1,0:T(8,128)S(1)} fusion(bf16[1024,4096]{0,1:T(8,128)(2,1)S(1)} %bitcast.58, bf16[1,4096,896]{2,1,0:T(8,128)(2,1)} %param.12), kind=kOutput, calls=%fused_computation.6 | convolution fusion | flops 7516192768 | bytes 19398656 | tf_op jit(solution)/shard_map/dot_general | solution.py:60
  159.7 11.1 %fusion.4 = f32[1024,896]{1,0:T(8,128)} fusion(bf16[1024,4096]{0,1:T(8,128)(2,1)S(1)} %bitcast.59, bf16[1,4096,896]{2,1,0:T(8,128)(2,1)S(1)} %bitcast.70), kind=kOutput, calls=%fused_computation.8 | convolution fusion | flops 7516192768 | bytes 19398656 | tf_op jit(solution)/shard_map/dot_general | solution.py:59
  170.8 13.8 %fusion.6 = f32[1024,8,2,256]{3,0,2,1:T(8,128)} fusion(bf16[8,2,256,896]{3,2,1,0:T(8,128)(2,1)S(1)} %bitcast.63, f32[1024,896]{1,0:T(8,128)S(1)} %fusion.2, f32[1024,896]{1,0:T(8,128)} %fusion.4), kind=kOutput, calls=%fused_computation.13 | convolution fusion | flops 7521697792 | bytes 31457280 | tf_op jit(solution)/shard_map/dot_general | solution.py:62
  184.6 10.1 %select_bitcast_fusion = f32[1024,8,256]{2,0,1:T(8,128)} fusion(f32[1024,8,2,256]{3,0,2,1:T(8,128)} %fusion.6, pred[]{:T(512)S(6)} %eq.43), kind=kLoop, calls=%fused_computation.5 | loop fusion | flops 2097152 | bytes 25165824 | tf_op jit(solution)/shard_map/jit(_where)/select_n | solution.py:65
  195.2 13.0 %collective-permute-done.1 = f32[1024,8,256]{2,0,1:T(8,128)S(1)} collective-permute-done((f32[1024,8,256]{2,0,1:T(8,128)}, f32[1024,8,256]{2,0,1:T(8,128)S(1)}, u32[]{:S(2)}, u32[]{:S(2)}) %collective-permute-start.1) | collective-permute-done | bytes 8388640 | tf_op jit(solution)/shard_map/ppermute | solution.py:32
  208.2 10.0 %fusion.1 = f32[1024,8,256]{2,0,1:T(8,128)} fusion(f32[1024,8,256]{2,0,1:T(8,128)S(1)} %collective-permute-done.1, f32[1024,8,2,256]{3,0,2,1:T(8,128)} %fusion.6, pred[]{:T(512)S(6)} %eq.43), kind=kLoop, calls=%fused_computation.4 | loop fusion | flops 4194304 | bytes 33554432 | tf_op jit(solution)/shard_map/add | solution.py:66
  218.2 112.7 %reduce-scatter.2.cloned.1.call-done = f32[1024,1,256]{2,0,1:T(8,128)} async-done(((f32[1024,8,256]{2,0,1:T(8,128)}), f32[1024,1,256]{2,0,1:T(8,128)}) %reduce-scatter.2.cloned.1.call-update) | async-done | bytes 1048592 | tf_op jit(solution)/shard_map/reduce_scatter | solution.py:67
  330.9 4.4 %all-to-all-start.1 = ((f32[8,128,256]{2,1,0:T(8,128)}), f32[8,128,256]{2,1,0:T(8,128)S(1)}, u32[]{:S(2)}, u32[]{:S(2)}) async-start(f32[8,128,256]{2,1,0:T(8,128)} %bitcast.65), calls=%async_computation.2 | async-start | bytes 2097152 | tf_op jit(solution)/shard_map/all_to_all | solution.py:69
  335.8 13.7 %all-to-all-done.1 = f32[8,128,256]{2,1,0:T(8,128)S(1)} async-done(((f32[8,128,256]{2,1,0:T(8,128)}), f32[8,128,256]{2,1,0:T(8,128)S(1)}, u32[]{:S(2)}, u32[]{:S(2)}) %all-to-all-start.1) | async-done | bytes 1048608 | tf_op jit(solution)/shard_map/all_to_all | solution.py:69
  349.5 1.6 gather_fusion
  351.4 0.7 multiply_reduce_fusion
  (38 shorter events, 3.1 us)
Async XLA Ops:
  6.5 114.8 %all-gather.2.cloned.1.call-start = ((), (), s32[]{:S(2)}) async-start(), calls=%async_computation.3 | async-start | bytes 4718592 | tf_op jit(solution)/shard_map/all_gather | solution.py:54
  54.3 276.6 %reduce-scatter.2.cloned.1.call-start = ((), (), s32[]{:S(2)}) async-start(), calls=%async_computation.4 | async-start | bytes 9437184 | tf_op jit(solution)/shard_map/reduce_scatter | solution.py:67
  127.8 10.8 %collective-permute-start = (bf16[8,1024,256]{1,2,0:T(8,128)(2,1)}, bf16[8,1024,256]{1,2,0:T(8,128)(2,1)}, u32[]{:S(2)}, u32[]{:S(2)}) collective-permute-start(bf16[8,1024,256]{1,2,0:T(8,128)(2,1)} %copy.54), channel_id=1, source_target_pairs={{0,1},{1,0},{2,3},{3,2},{4,5},{5,4},{6,7},{7,6},{8,9},{9,8},{10,11... | collective-permute-start | bytes 12582920 | tf_op jit(solution)/shard_map/ppermute | solution.py:32
  138.7 21.0 %slice-start.2 = ((s8[7340032]{0:T(1024)(128)(4,1)}), s8[4194304]{0:T(1024)(128)(4,1)S(1)}, s32[]{:S(2)}) async-start(s8[7340032]{0:T(1024)(128)(4,1)} %bitcast.69), calls=%async_computation.7 | async-start | bytes 8388608
  146.6 13.1 %slice-start.3 = ((s8[7340032]{0:T(1024)(128)(4,1)}), s8[3145728]{0:T(1024)(128)(4,1)S(1)}, s32[]{:S(2)}) async-start(s8[7340032]{0:T(1024)(128)(4,1)} %bitcast.69), calls=%async_computation.8 | async-start | bytes 6291456
  146.6 24.2 %slice-start = ((s8[7340032]{0:T(1024)(128)(4,1)}), s8[4194304]{0:T(1024)(128)(4,1)S(1)}, s32[]{:S(2)}) async-start(s8[7340032]{0:T(1024)(128)(4,1)} %bitcast.61), calls=%async_computation.5 | async-start | bytes 8388608
  159.7 11.1 %slice-start.1 = ((s8[7340032]{0:T(1024)(128)(4,1)}), s8[3145728]{0:T(1024)(128)(4,1)S(1)}, s32[]{:S(2)}) async-start(s8[7340032]{0:T(1024)(128)(4,1)} %bitcast.61), calls=%async_computation.6 | async-start | bytes 6291456
  194.6 13.5 %collective-permute-start.1 = (f32[1024,8,256]{2,0,1:T(8,128)}, f32[1024,8,256]{2,0,1:T(8,128)S(1)}, u32[]{:S(2)}, u32[]{:S(2)}) collective-permute-start(f32[1024,8,256]{2,0,1:T(8,128)} %select_bitcast_fusion), channel_id=1, source_target_pairs={{0,1},{1,0},{2,3},{3,2},{4,5},{5,4},{6,7},{7,6},{8,9},{9,8},{10,11... | collective-permute-start | bytes 25165832 | tf_op jit(solution)/shard_map/ppermute | solution.py:32
  218.2 117.4 %copy-start.1 = (f32[256,2]{0,1:T(2,128)S(1)}, f32[256,2]{0,1:T(2,128)}, u32[]{:S(2)}) copy-start(f32[256,2]{0,1:T(2,128)} %param.10) | copy-start | bytes 6148
  218.2 134.0 %copy-start = (bf16[256,256]{1,0:T(8,128)(2,1)S(1)}, bf16[256,256]{1,0:T(8,128)(2,1)}, u32[]{:S(2)}) copy-start(bf16[256,256]{1,0:T(8,128)(2,1)} %param.7) | copy-start | bytes 393220
  330.9 18.6 %all-to-all-start.1 = ((f32[8,128,256]{2,1,0:T(8,128)}), f32[8,128,256]{2,1,0:T(8,128)S(1)}, u32[]{:S(2)}, u32[]{:S(2)}) async-start(f32[8,128,256]{2,1,0:T(8,128)} %bitcast.65), calls=%async_computation.2 | async-start | bytes 2097152 | tf_op jit(solution)/shard_map/all_to_all | solution.py:69
Sparse Core Ops, SparseCore 0:
  54.4 66.8 all-gather.1
  218.3 112.5 reduce-scatter.1
